TPU v7x, 128 devices: a whole 4x4x4 slice. The times are simulated.
128 devices in a mesh: leaf: 8 (over x, core), prow: 4 (over z), pcol: 4 (over y).
Axes of the slice: x: 4, y: 4, z: 4, core: 2. Of those that a mesh axis runs over, the one named last changes fastest.
Arguments:
- subtree_factor: float32 [8, 2, 8, 256, 2048], P('leaf', None, None, 'prow', 'pcol'), may hold values from -0.09375 to 0.09375
- sub_linv: float32 [8, 2, 8, 256, 256], P('leaf', None, None, 'prow'), may hold values from -0.05 to 1.05
- sub_uinv: float32 [8, 2, 8, 256, 256], P('leaf', None, None, 'prow'), may hold values from -0.05 to 1.05
- lower_panel: float32 [8, 4, 256, 2, 2048], P('leaf', None, 'prow', None, 'pcol'), may hold values from -0.0234375 to 0.0234375
- upper_panel: float32 [8, 2, 8, 256, 1024], P('leaf', None, None, 'prow', 'pcol'), may hold values from -0.125 to 0.125
- panel_rows: int32 [8, 4, 2], P('leaf'), may hold values 0 or 1
- upper_level_factor: float32 [4, 256, 1024], P(None, 'prow', 'pcol'), may hold values from -0.125 to 0.125
- top_linv: float32 [4, 256, 256], P(None, 'prow'), may hold values from -0.05 to 1.05
- top_uinv: float32 [4, 256, 256], P(None, 'prow'), may hold values from -0.05 to 1.05
- sub_rhs: float32 [8, 2, 8, 256, 256], P('leaf', None, None, 'prow'), may hold values from -6 to 6
- top_rhs: float32 [4, 256, 256], P(None, 'prow', 'leaf'), may hold values from -6 to 6
Outputs:
- sub_solution: float32 [8, 2, 8, 256, 256], P('leaf', None, 'pcol')
- top_solution: float32 [4, 256, 256], P('pcol', None, 'leaf')
All inputs are finite; a program needn't handle non-finite values. No bound on the sum of `panel_rows` on one device may be relied on, other than what follows from the above.
Results may differ from a plain program's by a relative error of at most 0.00013.
Values sent between devices are 32-bit elements; how exact they have to be, the bound alone decides.
A program may use at most 128 MiB of HBM per device.

v0:
```python
import jax
import jax.numpy as jnp
from jax import lax
from jax.sharding import PartitionSpec as P

TOP_PRECISION = lax.Precision.HIGHEST


def block_order(block_count, forward):
    return range(block_count) if forward else range(block_count - 1, -1, -1)


def sweep_blocks(factor_row_block, inverses, right_side, coupling, owned_start, my_col, forward):
    groups, block_count, tile_rows, columns = right_side.shape
    block_rows = inverses.shape[3]
    owned_count = factor_row_block.shape[3] // block_rows
    solved = jnp.zeros((groups, block_count, block_rows, columns), jnp.float32)
    for sweep_step_index in block_order(block_count, forward):
        held_value_entries = lax.dynamic_slice_in_dim(solved, owned_start, owned_count, 1)
        held_value_entries = held_value_entries.reshape(groups, owned_count * block_rows, columns)
        partial_value = coupling[:, sweep_step_index] + jnp.einsum(
            "pht,ptj->phj",
            factor_row_block[:, sweep_step_index],
            held_value_entries,
            precision=TOP_PRECISION,
        )
        local_side = jnp.where(my_col == 0, right_side[:, sweep_step_index], 0.0) - partial_value
        inverse_part = jnp.einsum(
            "gab,gar->gbr", inverses[:, sweep_step_index], local_side, precision=TOP_PRECISION
        )
        block_value = lax.psum(inverse_part, ("prow", "pcol"))
        solved = solved.at[:, sweep_step_index].set(block_value)
    return solved


def per_device(
    subtree_factor,
    sub_linv,
    sub_uinv,
    lower_panel,
    upper_panel,
    panel_rows,
    upper_level_factor,
    top_linv,
    top_uinv,
    sub_rhs,
    top_rhs,
):
    my_row = lax.axis_index("prow")
    my_col = lax.axis_index("pcol")
    block_rows = sub_linv.shape[4]
    tile_rows = sub_rhs.shape[3]
    groups = sub_rhs.shape[1]
    block_count = sub_rhs.shape[2]
    sub_owned = subtree_factor.shape[4] // block_rows
    top_owned = upper_level_factor.shape[2] // block_rows
    present = panel_rows[0].astype(jnp.float32)
    linv_rows, uinv_rows, top_linv_rows, top_uinv_rows = (sub_linv, sub_uinv, top_linv, top_uinv)
    lower_sub = sweep_blocks(
        subtree_factor[0],
        linv_rows[0],
        sub_rhs[0],
        jnp.zeros(sub_rhs[0].shape, jnp.float32),
        my_col * sub_owned,
        my_col,
        True,
    )
    lower_owned = lax.dynamic_slice_in_dim(lower_sub, my_col * sub_owned, sub_owned, 1)
    lower_owned = lower_owned.reshape(groups, sub_owned * block_rows, lower_sub.shape[3])
    contrib_part = jnp.einsum(
        "tasm,ts,smr->tar", lower_panel[0], present, lower_owned, precision=TOP_PRECISION
    )
    contrib = lax.psum(contrib_part, "leaf")
    upper_level_side = lax.all_gather(top_rhs, "leaf", axis=2, tiled=True)
    upper_level_lower = sweep_blocks(
        upper_level_factor[None],
        top_linv_rows[None],
        upper_level_side[None],
        contrib[None],
        my_col * top_owned,
        my_col,
        True,
    )
    top_rows = lax.dynamic_slice_in_dim(upper_level_lower, my_row * tile_rows, tile_rows, 2)
    top_upper = sweep_blocks(
        upper_level_factor[None],
        top_uinv_rows[None],
        top_rows,
        jnp.zeros(top_rows.shape, jnp.float32),
        my_col * top_owned,
        my_col,
        False,
    )[0]
    top_out = lax.dynamic_slice_in_dim(
        top_upper, lax.axis_index("leaf") * top_rhs.shape[2], top_rhs.shape[2], 2
    )
    top_out = lax.dynamic_slice_in_dim(top_out, my_col * top_owned, top_owned, 0)
    top_mine = lax.dynamic_slice_in_dim(top_upper, my_col * top_owned, top_owned, 0)
    mask_mine = lax.dynamic_slice_in_dim(present, my_col * top_owned, top_owned, 0)
    upper_local = upper_panel[0].reshape(groups, block_count, tile_rows, top_owned, block_rows)
    coupling = jnp.einsum(
        "skatb,ts,tbr->skar", upper_local, mask_mine, top_mine, precision=TOP_PRECISION
    )
    sub_rows = lax.dynamic_slice_in_dim(lower_sub, my_row * tile_rows, tile_rows, 2)
    upper_sub = sweep_blocks(
        subtree_factor[0], uinv_rows[0], sub_rows, coupling, my_col * sub_owned, my_col, False
    )
    sub_out = lax.dynamic_slice_in_dim(upper_sub, my_col * sub_owned, sub_owned, 1)
    return (sub_out[None], top_out)


def solution(mesh):
    placed = (
        P("leaf", None, None, "prow", "pcol"),
        P("leaf", None, None, "prow", None),
        P("leaf", None, None, "prow", None),
        P("leaf", None, "prow", None, "pcol"),
        P("leaf", None, None, "prow", "pcol"),
        P("leaf", None, None),
        P(None, "prow", "pcol"),
        P(None, "prow", None),
        P(None, "prow", None),
        P("leaf", None, None, "prow", None),
        P(None, "prow", "leaf"),
    )
    return jax.shard_map(
        per_device,
        mesh=mesh,
        in_specs=placed,
        out_specs=(P("leaf", None, "pcol", None, None), P("pcol", None, "leaf")),
        check_vma=False,
    )
```

profile of v0, /device:TPU:0, one launch (start us, length us, event | category | flops | bytes accessed | tf_op | source)
XLA Modules:
  0.0 2303.5 jit_solution(17855429060302195027)
XLA Ops:
  7.2 2.4 copy.147
  9.7 2.3 copy.148
  13.5 2.3 convolution_bitcast_fusion.16
  15.9 88.4 %all-reduce.30.cloned.1.call-done = f32[2,1,256,256]{3,2,0,1:T(8,128)} async-done(((f32[2,1,256,256]{3,2,0,1:T(8,128)}), f32[2,1,256,256]{3,2,0,1:T(8,128)}) %all-reduce.30.cloned.1.call-update) | async-done | bytes 524304 | tf_op jit(solution)/shard_map/psum | solution.py:31
  107.2 2.3 convolution_bitcast_fusion.15
  109.6 3.4 scatter.80
  113.0 80.7 %all-reduce.32.cloned.1.call-done = f32[2,1,256,256]{3,2,0,1:T(8,128)} async-done(((f32[2,1,256,256]{3,2,0,1:T(8,128)}), f32[2,1,256,256]{3,2,0,1:T(8,128)}) %all-reduce.32.cloned.1.call-update) | async-done | bytes 524304 | tf_op jit(solution)/shard_map/psum | solution.py:31
  198.8 2.3 convolution_bitcast_fusion.14
  201.2 85.3 %all-reduce.34.cloned.1.call-done = f32[2,1,256,256]{3,2,0,1:T(8,128)} async-done(((f32[2,1,256,256]{3,2,0,1:T(8,128)}), f32[2,1,256,256]{3,2,0,1:T(8,128)}) %all-reduce.34.cloned.1.call-update) | async-done | bytes 524304 | tf_op jit(solution)/shard_map/psum | solution.py:31
  291.5 2.3 convolution_bitcast_fusion.13
  293.9 85.3 %all-reduce.36.cloned.1.call-done = f32[2,1,256,256]{3,2,0,1:T(8,128)} async-done(((f32[2,1,256,256]{3,2,0,1:T(8,128)}), f32[2,1,256,256]{3,2,0,1:T(8,128)}) %all-reduce.36.cloned.1.call-update) | async-done | bytes 524304 | tf_op jit(solution)/shard_map/psum | solution.py:31
  384.2 2.3 convolution_bitcast_fusion.12
  386.6 85.3 %all-reduce.38.cloned.1.call-done = f32[2,1,256,256]{3,2,0,1:T(8,128)} async-done(((f32[2,1,256,256]{3,2,0,1:T(8,128)}), f32[2,1,256,256]{3,2,0,1:T(8,128)}) %all-reduce.38.cloned.1.call-update) | async-done | bytes 524304 | tf_op jit(solution)/shard_map/psum | solution.py:31
  476.9 2.3 convolution_bitcast_fusion.11
  479.3 85.2 %all-reduce.40.cloned.1.call-done = f32[2,1,256,256]{3,2,0,1:T(8,128)} async-done(((f32[2,1,256,256]{3,2,0,1:T(8,128)}), f32[2,1,256,256]{3,2,0,1:T(8,128)}) %all-reduce.40.cloned.1.call-update) | async-done | bytes 524304 | tf_op jit(solution)/shard_map/psum | solution.py:31
  569.5 2.3 convolution_bitcast_fusion.10
  572.0 85.3 %all-reduce.42.cloned.1.call-done = f32[2,1,256,256]{3,2,0,1:T(8,128)} async-done(((f32[2,1,256,256]{3,2,0,1:T(8,128)}), f32[2,1,256,256]{3,2,0,1:T(8,128)}) %all-reduce.42.cloned.1.call-update) | async-done | bytes 524304 | tf_op jit(solution)/shard_map/psum | solution.py:31
  662.2 2.3 convolution_bitcast_fusion.9
  665.0 2.6 fusion.33
  667.6 82.2 %all-reduce.44.cloned.1.call-done = f32[2,1,256,256]{3,2,0,1:T(8,128)} async-done(((f32[2,1,256,256]{3,2,0,1:T(8,128)}), f32[2,1,256,256]{3,2,0,1:T(8,128)}) %all-reduce.44.cloned.1.call-update) | async-done | bytes 524304 | tf_op jit(solution)/shard_map/psum | solution.py:31
  755.1 14.6 all_gather.3
  771.9 42.9 %all-reduce.46.cloned.1.call-done = f32[1,4,64,256]{3,2,1,0:T(8,128)} async-done(((f32[1,4,64,256]{3,2,1,0:T(8,128)}), f32[1,4,64,256]{3,2,1,0:T(8,128)}) %all-reduce.46.cloned.1.call-update) | async-done | bytes 262160 | tf_op jit(solution)/shard_map/psum | solution.py:73
  816.8 85.7 %all-reduce.48.cloned.1.call-done = f32[1,1,256,256]{3,2,1,0:T(8,128)} async-done(((f32[1,1,256,256]{3,2,1,0:T(8,128)}), f32[1,1,256,256]{3,2,1,0:T(8,128)}) %all-reduce.48.cloned.1.call-update) | async-done | bytes 262160 | tf_op jit(solution)/shard_map/psum | solution.py:31
  907.9 82.4 %all-reduce.50.cloned.1.call-done = f32[1,1,256,256]{3,2,1,0:T(8,128)} async-done(((f32[1,1,256,256]{3,2,1,0:T(8,128)}), f32[1,1,256,256]{3,2,1,0:T(8,128)}) %all-reduce.50.cloned.1.call-update) | async-done | bytes 262160 | tf_op jit(solution)/shard_map/psum | solution.py:31
  995.2 84.5 %all-reduce.52.cloned.1.call-done = f32[1,1,256,256]{3,2,1,0:T(8,128)} async-done(((f32[1,1,256,256]{3,2,1,0:T(8,128)}), f32[1,1,256,256]{3,2,1,0:T(8,128)}) %all-reduce.52.cloned.1.call-update) | async-done | bytes 262160 | tf_op jit(solution)/shard_map/psum | solution.py:31
  1084.7 84.5 %all-reduce.54.cloned.1.call-done = f32[1,1,256,256]{3,2,1,0:T(8,128)} async-done(((f32[1,1,256,256]{3,2,1,0:T(8,128)}), f32[1,1,256,256]{3,2,1,0:T(8,128)}) %all-reduce.54.cloned.1.call-update) | async-done | bytes 262160 | tf_op jit(solution)/shard_map/psum | solution.py:31
  1173.0 84.5 %all-reduce.56.cloned.1.call-done = f32[1,1,256,256]{2,3,1,0:T(8,128)} async-done(((f32[1,1,256,256]{2,3,1,0:T(8,128)}), f32[1,1,256,256]{2,3,1,0:T(8,128)}) %all-reduce.56.cloned.1.call-update) | async-done | bytes 262160 | tf_op jit(solution)/shard_map/psum | solution.py:31
  1262.8 82.5 %all-reduce.58.cloned.1.call-done = f32[1,1,256,256]{2,3,1,0:T(8,128)} async-done(((f32[1,1,256,256]{2,3,1,0:T(8,128)}), f32[1,1,256,256]{2,3,1,0:T(8,128)}) %all-reduce.58.cloned.1.call-update) | async-done | bytes 262160 | tf_op jit(solution)/shard_map/psum | solution.py:31
  1350.3 84.5 %all-reduce.60.cloned.1.call-done = f32[1,1,256,256]{2,3,1,0:T(8,128)} async-done(((f32[1,1,256,256]{2,3,1,0:T(8,128)}), f32[1,1,256,256]{2,3,1,0:T(8,128)}) %all-reduce.60.cloned.1.call-update) | async-done | bytes 262160 | tf_op jit(solution)/shard_map/psum | solution.py:31
  1440.0 2.3 copy.146
  1442.3 82.0 %all-reduce.62.cloned.1.call-done = f32[1,256,256]{1,2,0:T(8,128)} async-done(((f32[1,256,256]{1,2,0:T(8,128)}), f32[1,256,256]{1,2,0:T(8,128)}) %all-reduce.62.cloned.1.call-update) | async-done | bytes 262160 | tf_op jit(solution)/shard_map/psum | solution.py:31
  1532.2 2.3 convolution_bitcast_fusion.8
  1534.6 85.1 %all-reduce.64.cloned.1.call-done = f32[2,1,256,256]{2,3,0,1:T(8,128)} async-done(((f32[2,1,256,256]{2,3,0,1:T(8,128)}), f32[2,1,256,256]{2,3,0,1:T(8,128)}) %all-reduce.64.cloned.1.call-update) | async-done | bytes 524304 | tf_op jit(solution)/shard_map/psum | solution.py:31
  1619.8 2.1 pad_dynamic-slice_fusion
  1621.9 2.6 copy.114
  1626.5 2.3 convolution_bitcast_fusion.7
  1629.1 3.4 scatter.106
  1632.5 81.6 %all-reduce.66.cloned.1.call-done = f32[2,1,256,256]{2,3,0,1:T(8,128)} async-done(((f32[2,1,256,256]{2,3,0,1:T(8,128)}), f32[2,1,256,256]{2,3,0,1:T(8,128)}) %all-reduce.66.cloned.1.call-update) | async-done | bytes 524304 | tf_op jit(solution)/shard_map/psum | solution.py:31
  1716.0 2.3 constant_dynamic-slice_fusion.7
  1718.2 2.5 copy.115
  1722.9 2.3 convolution_bitcast_fusion.6
  1725.3 85.2 %all-reduce.68.cloned.1.call-done = f32[2,1,256,256]{2,3,0,1:T(8,128)} async-done(((f32[2,1,256,256]{2,3,0,1:T(8,128)}), f32[2,1,256,256]{2,3,0,1:T(8,128)}) %all-reduce.68.cloned.1.call-update) | async-done | bytes 524304 | tf_op jit(solution)/shard_map/psum | solution.py:31
  1812.4 2.3 constant_dynamic-slice_fusion.6
  1814.6 2.5 copy.116
  1817.2 2.1 fusion.15
  1819.3 2.3 convolution_bitcast_fusion.5
  1821.7 85.2 %all-reduce.70.cloned.1.call-done = f32[2,1,256,256]{2,3,0,1:T(8,128)} async-done(((f32[2,1,256,256]{2,3,0,1:T(8,128)}), f32[2,1,256,256]{2,3,0,1:T(8,128)}) %all-reduce.70.cloned.1.call-update) | async-done | bytes 524304 | tf_op jit(solution)/shard_map/psum | solution.py:31
  1908.7 2.3 constant_dynamic-slice_fusion.5
  1911.0 2.5 copy.117
  1915.6 2.3 convolution_bitcast_fusion.4
  1918.0 85.2 %all-reduce.72.cloned.1.call-done = f32[2,1,256,256]{2,3,0,1:T(8,128)} async-done(((f32[2,1,256,256]{2,3,0,1:T(8,128)}), f32[2,1,256,256]{2,3,0,1:T(8,128)}) %all-reduce.72.cloned.1.call-update) | async-done | bytes 524304 | tf_op jit(solution)/shard_map/psum | solution.py:31
  2005.1 2.3 constant_dynamic-slice_fusion.4
  2007.4 2.5 copy.118
  2012.0 2.3 convolution_bitcast_fusion.3
  2014.4 85.3 %all-reduce.74.cloned.1.call-done = f32[2,1,256,256]{2,3,0,1:T(8,128)} async-done(((f32[2,1,256,256]{2,3,0,1:T(8,128)}), f32[2,1,256,256]{2,3,0,1:T(8,128)}) %all-reduce.74.cloned.1.call-update) | async-done | bytes 524304 | tf_op jit(solution)/shard_map/psum | solution.py:31
  2101.6 2.3 constant_dynamic-slice_fusion.3
  2103.8 2.5 copy.119
  2108.4 2.3 convolution_bitcast_fusion.2
  2110.9 85.2 %all-reduce.76.cloned.1.call-done = f32[2,1,256,256]{2,3,0,1:T(8,128)} async-done(((f32[2,1,256,256]{2,3,0,1:T(8,128)}), f32[2,1,256,256]{2,3,0,1:T(8,128)}) %all-reduce.76.cloned.1.call-update) | async-done | bytes 524304 | tf_op jit(solution)/shard_map/psum | solution.py:31
  2197.9 2.3 constant_dynamic-slice_fusion.2
  2200.2 2.5 copy.120
  2202.8 2.1 fusion.23
  2204.8 2.4 convolution_bitcast_fusion.1
  2208.7 83.8 %all-reduce.78.cloned.1.call-done = f32[2,1,256,256]{2,3,0,1:T(8,128)} async-done(((f32[2,1,256,256]{2,3,0,1:T(8,128)}), f32[2,1,256,256]{2,3,0,1:T(8,128)}) %all-reduce.78.cloned.1.call-update) | async-done | bytes 524304 | tf_op jit(solution)/shard_map/psum | solution.py:31
  (144 shorter events, 115.2 us)
Async XLA Ops:
  7.2 1521.5 %copy-start = (f32[1,2,8,64,256]{4,3,2,1,0:T(8,128)S(1)}, f32[1,2,8,64,256]{4,3,2,1,0:T(8,128)}, u32[]{:S(2)}) copy-start(f32[1,2,8,64,256]{4,3,2,1,0:T(8,128)} %param.63) | copy-start | bytes 3145732
  7.2 97.1 %all-reduce.30.cloned.1.call-start = ((), (), s32[]{:S(2)}) async-start(), calls=%async_computation | async-start | bytes 1048576 | tf_op jit(solution)/shard_map/psum | solution.py:31
  7.2 4.7 copy-start.3
  15.8 177.9 %all-reduce.32.cloned.1.call-start = ((), (), s32[]{:S(2)}) async-start(), calls=%async_computation.1 | async-start | bytes 1048576 | tf_op jit(solution)/shard_map/psum | solution.py:31
  109.6 176.9 %all-reduce.34.cloned.1.call-start = ((), (), s32[]{:S(2)}) async-start(), calls=%async_computation.2 | async-start | bytes 1048576 | tf_op jit(solution)/shard_map/psum | solution.py:31
  201.1 178.0 %all-reduce.36.cloned.1.call-start = ((), (), s32[]{:S(2)}) async-start(), calls=%async_computation.3 | async-start | bytes 1048576 | tf_op jit(solution)/shard_map/psum | solution.py:31
  293.9 178.0 %all-reduce.38.cloned.1.call-start = ((), (), s32[]{:S(2)}) async-start(), calls=%async_computation.4 | async-start | bytes 1048576 | tf_op jit(solution)/shard_map/psum | solution.py:31
  386.6 177.9 %all-reduce.40.cloned.1.call-start = ((), (), s32[]{:S(2)}) async-start(), calls=%async_computation.5 | async-start | bytes 1048576 | tf_op jit(solution)/shard_map/psum | solution.py:31
  479.3 177.9 %all-reduce.42.cloned.1.call-start = ((), (), s32[]{:S(2)}) async-start(), calls=%async_computation.6 | async-start | bytes 1048576 | tf_op jit(solution)/shard_map/psum | solution.py:31
  571.9 92.9 %copy-start.6 = (s32[1,4,2]{1,2,0:T(2,128)S(1)}, s32[1,4,2]{1,2,0:T(2,128)}, u32[]{:S(2)}) copy-start(s32[1,4,2]{1,2,0:T(2,128)} %param.64) | copy-start | bytes 100
  571.9 93.0 %copy-start.5 = (f32[4,64,32]{1,2,0:T(8,128)S(1)}, f32[4,64,32]{1,2,0:T(8,128)}, u32[]{:S(2)}) copy-start(f32[4,64,32]{1,2,0:T(8,128)} %param.69) | copy-start | bytes 98308
  571.9 177.9 %all-reduce.44.cloned.1.call-start = ((), (), s32[]{:S(2)}) async-start(), calls=%async_computation.7 | async-start | bytes 1048576 | tf_op jit(solution)/shard_map/psum | solution.py:31
  664.6 150.2 %all-reduce.46.cloned.1.call-start = ((), (), s32[]{:S(2)}) async-start(), calls=%async_computation.8 | async-start | bytes 524288 | tf_op jit(solution)/shard_map/psum | solution.py:73
  749.8 3.4 copy-start.1
  755.0 147.5 %all-reduce.48.cloned.1.call-start = ((), (), s32[]{:S(2)}) async-start(), calls=%async_computation.9 | async-start | bytes 524288 | tf_op jit(solution)/shard_map/psum | solution.py:31
  816.8 173.4 %all-reduce.50.cloned.1.call-start = ((), (), s32[]{:S(2)}) async-start(), calls=%async_computation.10 | async-start | bytes 524288 | tf_op jit(solution)/shard_map/psum | solution.py:31
  905.8 173.9 %all-reduce.52.cloned.1.call-start = ((), (), s32[]{:S(2)}) async-start(), calls=%async_computation.11 | async-start | bytes 524288 | tf_op jit(solution)/shard_map/psum | solution.py:31
  995.1 174.0 %all-reduce.54.cloned.1.call-start = ((), (), s32[]{:S(2)}) async-start(), calls=%async_computation.12 | async-start | bytes 524288 | tf_op jit(solution)/shard_map/psum | solution.py:31
  1082.6 264.3 %copy-start.4 = (f32[4,64,256]{2,1,0:T(8,128)S(1)}, f32[4,64,256]{2,1,0:T(8,128)}, u32[]{:S(2)}) copy-start(f32[4,64,256]{2,1,0:T(8,128)} %param.65) | copy-start | bytes 786436
  1084.7 172.8 %all-reduce.56.cloned.1.call-start = ((), (), s32[]{:S(2)}) async-start(), calls=%async_computation.13 | async-start | bytes 524288 | tf_op jit(solution)/shard_map/psum | solution.py:31
  1172.9 172.3 %all-reduce.58.cloned.1.call-start = ((), (), s32[]{:S(2)}) async-start(), calls=%async_computation.14 | async-start | bytes 524288 | tf_op jit(solution)/shard_map/psum | solution.py:31
  1260.7 174.1 %all-reduce.60.cloned.1.call-start = ((), (), s32[]{:S(2)}) async-start(), calls=%async_computation.15 | async-start | bytes 524288 | tf_op jit(solution)/shard_map/psum | solution.py:31
  1350.2 174.0 %all-reduce.62.cloned.1.call-start = ((), (), s32[]{:S(2)}) async-start(), calls=%async_computation.16 | async-start | bytes 524288 | tf_op jit(solution)/shard_map/psum | solution.py:31
  1439.8 180.0 %all-reduce.64.cloned.1.call-start = ((), (), s32[]{:S(2)}) async-start(), calls=%async_computation.17 | async-start | bytes 1048576 | tf_op jit(solution)/shard_map/psum | solution.py:31
  1529.9 1.1 copy-start.2
  1534.6 179.5 %all-reduce.66.cloned.1.call-start = ((), (), s32[]{:S(2)}) async-start(), calls=%async_computation.18 | async-start | bytes 1048576 | tf_op jit(solution)/shard_map/psum | solution.py:31
  1628.9 181.6 %all-reduce.68.cloned.1.call-start = ((), (), s32[]{:S(2)}) async-start(), calls=%async_computation.19 | async-start | bytes 1048576 | tf_op jit(solution)/shard_map/psum | solution.py:31
  1725.2 181.6 %all-reduce.70.cloned.1.call-start = ((), (), s32[]{:S(2)}) async-start(), calls=%async_computation.20 | async-start | bytes 1048576 | tf_op jit(solution)/shard_map/psum | solution.py:31
  1821.6 181.6 %all-reduce.72.cloned.1.call-start = ((), (), s32[]{:S(2)}) async-start(), calls=%async_computation.21 | async-start | bytes 1048576 | tf_op jit(solution)/shard_map/psum | solution.py:31
  1918.0 181.7 %all-reduce.74.cloned.1.call-start = ((), (), s32[]{:S(2)}) async-start(), calls=%async_computation.22 | async-start | bytes 1048576 | tf_op jit(solution)/shard_map/psum | solution.py:31
  2014.3 181.7 %all-reduce.76.cloned.1.call-start = ((), (), s32[]{:S(2)}) async-start(), calls=%async_computation.23 | async-start | bytes 1048576 | tf_op jit(solution)/shard_map/psum | solution.py:31
  2110.8 181.7 %all-reduce.78.cloned.1.call-start = ((), (), s32[]{:S(2)}) async-start(), calls=%async_computation.24 | async-start | bytes 1048576 | tf_op jit(solution)/shard_map/psum | solution.py:31
Sparse Core Ops, SparseCore 0:
  15.9 88.3 all-reduce.29
  109.7 84.0 all-reduce.31
  201.3 85.1 all-reduce.33
  294.0 85.1 all-reduce.35
  386.7 85.1 all-reduce.37
  479.4 85.0 all-reduce.39
  572.0 85.1 all-reduce.41
  664.7 85.0 all-reduce.43
  755.1 59.5 all-reduce.45
  818.3 84.1 all-reduce.47
  905.9 84.2 all-reduce.49
  995.3 84.3 all-reduce.51
  1084.8 84.3 all-reduce.53
  1173.1 84.3 all-reduce.55
  1260.8 84.3 all-reduce.57
  1350.4 84.3 all-reduce.59
  1439.9 84.3 all-reduce.61
  1534.7 85.0 all-reduce.63
  1629.0 85.0 all-reduce.65
  1725.3 85.0 all-reduce.67
  1821.7 85.0 all-reduce.69
  1918.1 85.0 all-reduce.71
  2014.5 85.1 all-reduce.73
  2110.9 85.0 all-reduce.75
  2207.4 85.0 all-reduce.77
where the time goes:
time: 2310 us; the launch traced here: 2300 us
  waiting for transfers between devices  2070 us (90%)
  local copies, waits for them, and re-layouts  108 us (5%)
  matrix products  93 us (4%)
    psum x24, waiting for transfers between devices, sweep_blocks(): block_value = lax.psum(inverse_part, ('prow', 'pcol'))  2020 us
    dot_general x24, matrix products, sweep_blocks(): jnp.einsum('gab,gar->gbr', inverses[:, sweep_step_index], local_side, pre...  53.3 us
    scatter x24, local copies, waits for them, and re-layouts, sweep_blocks(): solved = solved.at[:, sweep_step_index].set(block_value)  47.2 us
  transfers between devices with their start and end apart: 25, of which 25 were waited for; matrix products, arithmetic and copies ran while one was open for 1% of the time, Pallas kernels for 0%

commit v1 on v0

--- a/solution.py
+++ b/solution.py
@@ -28,7 +28,7 @@
         inverse_part = jnp.einsum(
             "gab,gar->gbr", inverses[:, sweep_step_index], local_side, precision=TOP_PRECISION
         )
-        block_value = lax.psum(inverse_part, ("prow", "pcol"))
+        block_value = lax.psum(lax.psum(inverse_part, axis_name="pcol"), axis_name="prow")
         solved = solved.at[:, sweep_step_index].set(block_value)
     return solved
 

time: 2310 us -> 2400 us (1.039)
  waiting for transfers between devices: 2070 us -> 2160 us
    psum x24 -> x48, waiting for transfers between devices: 2020 us -> 2120 us  [the longest x24 1080 us: sweep_blocks(): lax.psum(lax.psum(inverse_part, axis_name='pcol'), axis_name='prow')]
  transfers between devices with their start and end apart: 25 -> 49, of which waited for: 25 -> 49; matrix products, arithmetic and copies ran while one was open for 1% -> 1% of each run, Pallas kernels for 0% -> 0%
where the time goes in v1:
time: 2400 us
  waiting for transfers between devices  2160 us (90%)
  local copies, waits for them, and re-layouts  108 us (4%)
  matrix products  93 us (4%)
    psum x24, waiting for transfers between devices, sweep_blocks(): lax.psum(lax.psum(inverse_part, axis_name='pcol'), axis_name='prow')  1080 us
    psum x24, waiting for transfers between devices, sweep_blocks(): lax.psum(inverse_part, axis_name='pcol')  1040 us
    dot_general x24, matrix products, sweep_blocks(): jnp.einsum('gab,gar->gbr', inverses[:, sweep_step_index], local_side, pre...  53.4 us
  transfers between devices with their start and end apart: 49, of which 49 were waited for; matrix products, arithmetic and copies ran while one was open for 1% of the time, Pallas kernels for 0%

profile of v1, /device:TPU:0, one launch (start us, length us, event | category | flops | bytes accessed | tf_op | source)
XLA Modules:
  0.0 2400.3 jit_solution(1151311151271409800)
XLA Ops:
  7.2 2.4 copy.147
  15.9 45.6 %all-reduce.54.cloned.1.call-done = f32[2,256,256]{2,1,0:T(8,128)} async-done(((f32[2,256,256]{2,1,0:T(8,128)}), f32[2,256,256]{2,1,0:T(8,128)}) %all-reduce.54.cloned.1.call-update) | async-done | bytes 524304 | tf_op jit(solution)/shard_map/psum | solution.py:31
  61.6 46.2 %all-reduce.56.cloned.1.call-done = f32[2,1,256,256]{3,2,0,1:T(8,128)} async-done(((f32[2,1,256,256]{3,2,0,1:T(8,128)}), f32[2,1,256,256]{3,2,0,1:T(8,128)}) %all-reduce.56.cloned.1.call-update) | async-done | bytes 524304 | tf_op jit(solution)/shard_map/psum | solution.py:31
  113.2 42.8 %all-reduce.58.cloned.1.call-done = f32[2,256,256]{2,1,0:T(8,128)} async-done(((f32[2,256,256]{2,1,0:T(8,128)}), f32[2,256,256]{2,1,0:T(8,128)}) %all-reduce.58.cloned.1.call-update) | async-done | bytes 524304 | tf_op jit(solution)/shard_map/psum | solution.py:31
  156.0 3.4 scatter.80
  159.4 42.7 %all-reduce.60.cloned.1.call-done = f32[2,1,256,256]{3,2,0,1:T(8,128)} async-done(((f32[2,1,256,256]{3,2,0,1:T(8,128)}), f32[2,1,256,256]{3,2,0,1:T(8,128)}) %all-reduce.60.cloned.1.call-update) | async-done | bytes 524304 | tf_op jit(solution)/shard_map/psum | solution.py:31
  209.5 43.8 %all-reduce.62.cloned.1.call-done = f32[2,256,256]{2,1,0:T(8,128)} async-done(((f32[2,256,256]{2,1,0:T(8,128)}), f32[2,256,256]{2,1,0:T(8,128)}) %all-reduce.62.cloned.1.call-update) | async-done | bytes 524304 | tf_op jit(solution)/shard_map/psum | solution.py:31
  253.4 46.1 %all-reduce.64.cloned.1.call-done = f32[2,1,256,256]{3,2,0,1:T(8,128)} async-done(((f32[2,1,256,256]{3,2,0,1:T(8,128)}), f32[2,1,256,256]{3,2,0,1:T(8,128)}) %all-reduce.64.cloned.1.call-update) | async-done | bytes 524304 | tf_op jit(solution)/shard_map/psum | solution.py:31
  306.9 43.8 %all-reduce.66.cloned.1.call-done = f32[2,256,256]{2,1,0:T(8,128)} async-done(((f32[2,256,256]{2,1,0:T(8,128)}), f32[2,256,256]{2,1,0:T(8,128)}) %all-reduce.66.cloned.1.call-update) | async-done | bytes 524304 | tf_op jit(solution)/shard_map/psum | solution.py:31
  350.8 46.2 %all-reduce.68.cloned.1.call-done = f32[2,1,256,256]{3,2,0,1:T(8,128)} async-done(((f32[2,1,256,256]{3,2,0,1:T(8,128)}), f32[2,1,256,256]{3,2,0,1:T(8,128)}) %all-reduce.68.cloned.1.call-update) | async-done | bytes 524304 | tf_op jit(solution)/shard_map/psum | solution.py:31
  404.4 43.8 %all-reduce.70.cloned.1.call-done = f32[2,256,256]{2,1,0:T(8,128)} async-done(((f32[2,256,256]{2,1,0:T(8,128)}), f32[2,256,256]{2,1,0:T(8,128)}) %all-reduce.70.cloned.1.call-update) | async-done | bytes 524304 | tf_op jit(solution)/shard_map/psum | solution.py:31
  448.3 46.1 %all-reduce.72.cloned.1.call-done = f32[2,1,256,256]{3,2,0,1:T(8,128)} async-done(((f32[2,1,256,256]{3,2,0,1:T(8,128)}), f32[2,1,256,256]{3,2,0,1:T(8,128)}) %all-reduce.72.cloned.1.call-update) | async-done | bytes 524304 | tf_op jit(solution)/shard_map/psum | solution.py:31
  501.8 43.8 %all-reduce.74.cloned.1.call-done = f32[2,256,256]{2,1,0:T(8,128)} async-done(((f32[2,256,256]{2,1,0:T(8,128)}), f32[2,256,256]{2,1,0:T(8,128)}) %all-reduce.74.cloned.1.call-update) | async-done | bytes 524304 | tf_op jit(solution)/shard_map/psum | solution.py:31
  545.7 46.1 %all-reduce.76.cloned.1.call-done = f32[2,1,256,256]{3,2,0,1:T(8,128)} async-done(((f32[2,1,256,256]{3,2,0,1:T(8,128)}), f32[2,1,256,256]{3,2,0,1:T(8,128)}) %all-reduce.76.cloned.1.call-update) | async-done | bytes 524304 | tf_op jit(solution)/shard_map/psum | solution.py:31
  599.2 43.8 %all-reduce.78.cloned.1.call-done = f32[2,256,256]{2,1,0:T(8,128)} async-done(((f32[2,256,256]{2,1,0:T(8,128)}), f32[2,256,256]{2,1,0:T(8,128)}) %all-reduce.78.cloned.1.call-update) | async-done | bytes 524304 | tf_op jit(solution)/shard_map/psum | solution.py:31
  643.3 45.9 %all-reduce.80.cloned.1.call-done = f32[2,1,256,256]{3,2,0,1:T(8,128)} async-done(((f32[2,1,256,256]{3,2,0,1:T(8,128)}), f32[2,1,256,256]{3,2,0,1:T(8,128)}) %all-reduce.80.cloned.1.call-update) | async-done | bytes 524304 | tf_op jit(solution)/shard_map/psum | solution.py:31
  696.5 43.8 %all-reduce.82.cloned.1.call-done = f32[2,256,256]{2,1,0:T(8,128)} async-done(((f32[2,256,256]{2,1,0:T(8,128)}), f32[2,256,256]{2,1,0:T(8,128)}) %all-reduce.82.cloned.1.call-update) | async-done | bytes 524304 | tf_op jit(solution)/shard_map/psum | solution.py:31
  740.6 2.6 fusion.33
  743.2 43.3 %all-reduce.84.cloned.1.call-done = f32[2,1,256,256]{3,2,0,1:T(8,128)} async-done(((f32[2,1,256,256]{3,2,0,1:T(8,128)}), f32[2,1,256,256]{3,2,0,1:T(8,128)}) %all-reduce.84.cloned.1.call-update) | async-done | bytes 524304 | tf_op jit(solution)/shard_map/psum | solution.py:31
  791.8 14.5 all_gather.3
  808.5 44.2 %all-reduce.86.cloned.1.call-done = f32[1,4,64,256]{3,2,1,0:T(8,128)} async-done(((f32[1,4,64,256]{3,2,1,0:T(8,128)}), f32[1,4,64,256]{3,2,1,0:T(8,128)}) %all-reduce.86.cloned.1.call-update) | async-done | bytes 262160 | tf_op jit(solution)/shard_map/psum | solution.py:73
  854.8 41.6 %all-reduce.88.cloned.1.call-done = f32[1,256,256]{2,1,0:T(8,128)} async-done(((f32[1,256,256]{2,1,0:T(8,128)}), f32[1,256,256]{2,1,0:T(8,128)}) %all-reduce.88.cloned.1.call-update) | async-done | bytes 262160 | tf_op jit(solution)/shard_map/psum | solution.py:31
  896.5 44.9 %all-reduce.90.cloned.1.call-done = f32[1,1,256,256]{3,2,1,0:T(8,128)} async-done(((f32[1,1,256,256]{3,2,1,0:T(8,128)}), f32[1,1,256,256]{3,2,1,0:T(8,128)}) %all-reduce.90.cloned.1.call-update) | async-done | bytes 262160 | tf_op jit(solution)/shard_map/psum | solution.py:31
  944.7 42.2 %all-reduce.92.cloned.1.call-done = f32[1,256,256]{2,1,0:T(8,128)} async-done(((f32[1,256,256]{2,1,0:T(8,128)}), f32[1,256,256]{2,1,0:T(8,128)}) %all-reduce.92.cloned.1.call-update) | async-done | bytes 262160 | tf_op jit(solution)/shard_map/psum | solution.py:31
  989.0 42.9 %all-reduce.94.cloned.1.call-done = f32[1,1,256,256]{3,2,1,0:T(8,128)} async-done(((f32[1,1,256,256]{3,2,1,0:T(8,128)}), f32[1,1,256,256]{3,2,1,0:T(8,128)}) %all-reduce.94.cloned.1.call-update) | async-done | bytes 262160 | tf_op jit(solution)/shard_map/psum | solution.py:31
  1036.8 42.3 %all-reduce.96.cloned.1.call-done = f32[1,256,256]{2,1,0:T(8,128)} async-done(((f32[1,256,256]{2,1,0:T(8,128)}), f32[1,256,256]{2,1,0:T(8,128)}) %all-reduce.96.cloned.1.call-update) | async-done | bytes 262160 | tf_op jit(solution)/shard_map/psum | solution.py:31
  1079.2 44.9 %all-reduce.98.cloned.1.call-done = f32[1,1,256,256]{3,2,1,0:T(8,128)} async-done(((f32[1,1,256,256]{3,2,1,0:T(8,128)}), f32[1,1,256,256]{3,2,1,0:T(8,128)}) %all-reduce.98.cloned.1.call-update) | async-done | bytes 262160 | tf_op jit(solution)/shard_map/psum | solution.py:31
  1129.1 42.3 %all-reduce.100.cloned.1.call-done = f32[1,256,256]{2,1,0:T(8,128)} async-done(((f32[1,256,256]{2,1,0:T(8,128)}), f32[1,256,256]{2,1,0:T(8,128)}) %all-reduce.100.cloned.1.call-update) | async-done | bytes 262160 | tf_op jit(solution)/shard_map/psum | solution.py:31
  1171.5 44.9 %all-reduce.102.cloned.1.call-done = f32[1,1,256,256]{3,2,1,0:T(8,128)} async-done(((f32[1,1,256,256]{3,2,1,0:T(8,128)}), f32[1,1,256,256]{3,2,1,0:T(8,128)}) %all-reduce.102.cloned.1.call-update) | async-done | bytes 262160 | tf_op jit(solution)/shard_map/psum | solution.py:31
  1220.2 42.3 %all-reduce.104.cloned.1.call-done = f32[1,256,256]{1,2,0:T(8,128)} async-done(((f32[1,256,256]{1,2,0:T(8,128)}), f32[1,256,256]{1,2,0:T(8,128)}) %all-reduce.104.cloned.1.call-update) | async-done | bytes 262160 | tf_op jit(solution)/shard_map/psum | solution.py:31
  1262.6 44.7 %all-reduce.106.cloned.1.call-done = f32[1,1,256,256]{2,3,1,0:T(8,128)} async-done(((f32[1,1,256,256]{2,3,1,0:T(8,128)}), f32[1,1,256,256]{2,3,1,0:T(8,128)}) %all-reduce.106.cloned.1.call-update) | async-done | bytes 262160 | tf_op jit(solution)/shard_map/psum | solution.py:31
  1310.6 42.4 %all-reduce.108.cloned.1.call-done = f32[1,256,256]{1,2,0:T(8,128)} async-done(((f32[1,256,256]{1,2,0:T(8,128)}), f32[1,256,256]{1,2,0:T(8,128)}) %all-reduce.108.cloned.1.call-update) | async-done | bytes 262160 | tf_op jit(solution)/shard_map/psum | solution.py:31
  1355.0 42.9 %all-reduce.110.cloned.1.call-done = f32[1,1,256,256]{2,3,1,0:T(8,128)} async-done(((f32[1,1,256,256]{2,3,1,0:T(8,128)}), f32[1,1,256,256]{2,3,1,0:T(8,128)}) %all-reduce.110.cloned.1.call-update) | async-done | bytes 262160 | tf_op jit(solution)/shard_map/psum | solution.py:31
  1402.9 42.3 %all-reduce.112.cloned.1.call-done = f32[1,256,256]{1,2,0:T(8,128)} async-done(((f32[1,256,256]{1,2,0:T(8,128)}), f32[1,256,256]{1,2,0:T(8,128)}) %all-reduce.112.cloned.1.call-update) | async-done | bytes 262160 | tf_op jit(solution)/shard_map/psum | solution.py:31
  1445.3 44.9 %all-reduce.114.cloned.1.call-done = f32[1,1,256,256]{2,3,1,0:T(8,128)} async-done(((f32[1,1,256,256]{2,3,1,0:T(8,128)}), f32[1,1,256,256]{2,3,1,0:T(8,128)}) %all-reduce.114.cloned.1.call-update) | async-done | bytes 262160 | tf_op jit(solution)/shard_map/psum | solution.py:31
  1495.2 42.3 %all-reduce.116.cloned.1.call-done = f32[1,256,256]{1,2,0:T(8,128)} async-done(((f32[1,256,256]{1,2,0:T(8,128)}), f32[1,256,256]{1,2,0:T(8,128)}) %all-reduce.116.cloned.1.call-update) | async-done | bytes 262160 | tf_op jit(solution)/shard_map/psum | solution.py:31
  1540.1 42.2 %all-reduce.118.cloned.1.call-done = f32[1,256,256]{1,2,0:T(8,128)} async-done(((f32[1,256,256]{1,2,0:T(8,128)}), f32[1,256,256]{1,2,0:T(8,128)}) %all-reduce.118.cloned.1.call-update) | async-done | bytes 262160 | tf_op jit(solution)/shard_map/psum | solution.py:31
  1592.7 43.6 %all-reduce.120.cloned.1.call-done = f32[2,256,256]{1,2,0:T(8,128)} async-done(((f32[2,256,256]{1,2,0:T(8,128)}), f32[2,256,256]{1,2,0:T(8,128)}) %all-reduce.120.cloned.1.call-update) | async-done | bytes 524304 | tf_op jit(solution)/shard_map/psum | solution.py:31
  1636.6 46.0 %all-reduce.122.cloned.1.call-done = f32[2,1,256,256]{2,3,0,1:T(8,128)} async-done(((f32[2,1,256,256]{2,3,0,1:T(8,128)}), f32[2,1,256,256]{2,3,0,1:T(8,128)}) %all-reduce.122.cloned.1.call-update) | async-done | bytes 524304 | tf_op jit(solution)/shard_map/psum | solution.py:31
  1684.7 2.6 copy.114
  1691.7 43.8 %all-reduce.124.cloned.1.call-done = f32[2,256,256]{1,2,0:T(8,128)} async-done(((f32[2,256,256]{1,2,0:T(8,128)}), f32[2,256,256]{1,2,0:T(8,128)}) %all-reduce.124.cloned.1.call-update) | async-done | bytes 524304 | tf_op jit(solution)/shard_map/psum | solution.py:31
  1735.6 3.4 scatter.106
  1739.0 42.7 %all-reduce.126.cloned.1.call-done = f32[2,1,256,256]{2,3,0,1:T(8,128)} async-done(((f32[2,1,256,256]{2,3,0,1:T(8,128)}), f32[2,1,256,256]{2,3,0,1:T(8,128)}) %all-reduce.126.cloned.1.call-update) | async-done | bytes 524304 | tf_op jit(solution)/shard_map/psum | solution.py:31
  1785.9 2.5 copy.115
  1790.5 2.4 convolution_bitcast_fusion.6
  1792.9 43.8 %all-reduce.128.cloned.1.call-done = f32[2,256,256]{1,2,0:T(8,128)} async-done(((f32[2,256,256]{1,2,0:T(8,128)}), f32[2,256,256]{1,2,0:T(8,128)}) %all-reduce.128.cloned.1.call-update) | async-done | bytes 524304 | tf_op jit(solution)/shard_map/psum | solution.py:31
  1836.8 46.1 %all-reduce.130.cloned.1.call-done = f32[2,1,256,256]{2,3,0,1:T(8,128)} async-done(((f32[2,1,256,256]{2,3,0,1:T(8,128)}), f32[2,1,256,256]{2,3,0,1:T(8,128)}) %all-reduce.130.cloned.1.call-update) | async-done | bytes 524304 | tf_op jit(solution)/shard_map/psum | solution.py:31
  1887.1 2.5 copy.116
  1894.1 43.8 %all-reduce.132.cloned.1.call-done = f32[2,256,256]{1,2,0:T(8,128)} async-done(((f32[2,256,256]{1,2,0:T(8,128)}), f32[2,256,256]{1,2,0:T(8,128)}) %all-reduce.132.cloned.1.call-update) | async-done | bytes 524304 | tf_op jit(solution)/shard_map/psum | solution.py:31
  1938.0 46.2 %all-reduce.134.cloned.1.call-done = f32[2,1,256,256]{2,3,0,1:T(8,128)} async-done(((f32[2,1,256,256]{2,3,0,1:T(8,128)}), f32[2,1,256,256]{2,3,0,1:T(8,128)}) %all-reduce.134.cloned.1.call-update) | async-done | bytes 524304 | tf_op jit(solution)/shard_map/psum | solution.py:31
  1988.4 2.5 copy.117
  1995.4 43.8 %all-reduce.136.cloned.1.call-done = f32[2,256,256]{1,2,0:T(8,128)} async-done(((f32[2,256,256]{1,2,0:T(8,128)}), f32[2,256,256]{1,2,0:T(8,128)}) %all-reduce.136.cloned.1.call-update) | async-done | bytes 524304 | tf_op jit(solution)/shard_map/psum | solution.py:31
  2039.3 46.1 %all-reduce.138.cloned.1.call-done = f32[2,1,256,256]{2,3,0,1:T(8,128)} async-done(((f32[2,1,256,256]{2,3,0,1:T(8,128)}), f32[2,1,256,256]{2,3,0,1:T(8,128)}) %all-reduce.138.cloned.1.call-update) | async-done | bytes 524304 | tf_op jit(solution)/shard_map/psum | solution.py:31
  2089.5 2.5 copy.118
  2094.2 2.4 convolution_bitcast_fusion.3
  2096.6 43.8 %all-reduce.140.cloned.1.call-done = f32[2,256,256]{1,2,0:T(8,128)} async-done(((f32[2,256,256]{1,2,0:T(8,128)}), f32[2,256,256]{1,2,0:T(8,128)}) %all-reduce.140.cloned.1.call-update) | async-done | bytes 524304 | tf_op jit(solution)/shard_map/psum | solution.py:31
  2140.5 46.1 %all-reduce.142.cloned.1.call-done = f32[2,1,256,256]{2,3,0,1:T(8,128)} async-done(((f32[2,1,256,256]{2,3,0,1:T(8,128)}), f32[2,1,256,256]{2,3,0,1:T(8,128)}) %all-reduce.142.cloned.1.call-update) | async-done | bytes 524304 | tf_op jit(solution)/shard_map/psum | solution.py:31
  2190.7 2.5 copy.119
  2197.8 43.8 %all-reduce.144.cloned.1.call-done = f32[2,256,256]{1,2,0:T(8,128)} async-done(((f32[2,256,256]{1,2,0:T(8,128)}), f32[2,256,256]{1,2,0:T(8,128)}) %all-reduce.144.cloned.1.call-update) | async-done | bytes 524304 | tf_op jit(solution)/shard_map/psum | solution.py:31
  2241.6 46.1 %all-reduce.146.cloned.1.call-done = f32[2,1,256,256]{2,3,0,1:T(8,128)} async-done(((f32[2,1,256,256]{2,3,0,1:T(8,128)}), f32[2,1,256,256]{2,3,0,1:T(8,128)}) %all-reduce.146.cloned.1.call-update) | async-done | bytes 524304 | tf_op jit(solution)/shard_map/psum | solution.py:31
  2291.9 2.5 copy.120
  2296.5 2.4 convolution_bitcast_fusion.1
  2299.0 43.8 %all-reduce.148.cloned.1.call-done = f32[2,256,256]{1,2,0:T(8,128)} async-done(((f32[2,256,256]{1,2,0:T(8,128)}), f32[2,256,256]{1,2,0:T(8,128)}) %all-reduce.148.cloned.1.call-update) | async-done | bytes 524304 | tf_op jit(solution)/shard_map/psum | solution.py:31
  2344.2 44.7 %all-reduce.150.cloned.1.call-done = f32[2,1,256,256]{2,3,0,1:T(8,128)} async-done(((f32[2,1,256,256]{2,3,0,1:T(8,128)}), f32[2,1,256,256]{2,3,0,1:T(8,128)}) %all-reduce.150.cloned.1.call-update) | async-done | bytes 524304 | tf_op jit(solution)/shard_map/psum | solution.py:31
  (216 shorter events, 171.5 us)
Async XLA Ops:
  7.2 1579.6 %copy-start = (f32[1,2,8,64,256]{4,3,2,1,0:T(8,128)S(1)}, f32[1,2,8,64,256]{4,3,2,1,0:T(8,128)}, u32[]{:S(2)}) copy-start(f32[1,2,8,64,256]{4,3,2,1,0:T(8,128)} %param.63) | copy-start | bytes 3145732
  7.2 54.4 %all-reduce.54.cloned.1.call-start = ((), (), s32[]{:S(2)}) async-start(), calls=%async_computation | async-start | bytes 1048576 | tf_op jit(solution)/shard_map/psum | solution.py:31
  7.2 4.7 copy-start.3
  15.8 92.0 %all-reduce.56.cloned.1.call-start = ((), (), s32[]{:S(2)}) async-start(), calls=%async_computation.1 | async-start | bytes 1048576 | tf_op jit(solution)/shard_map/psum | solution.py:31
  61.6 94.4 %all-reduce.58.cloned.1.call-start = ((), (), s32[]{:S(2)}) async-start(), calls=%async_computation.2 | async-start | bytes 1048576 | tf_op jit(solution)/shard_map/psum | solution.py:31
  113.1 89.0 %all-reduce.60.cloned.1.call-start = ((), (), s32[]{:S(2)}) async-start(), calls=%async_computation.3 | async-start | bytes 1048576 | tf_op jit(solution)/shard_map/psum | solution.py:31
  156.0 97.4 %all-reduce.62.cloned.1.call-start = ((), (), s32[]{:S(2)}) async-start(), calls=%async_computation.4 | async-start | bytes 1048576 | tf_op jit(solution)/shard_map/psum | solution.py:31
  209.5 90.0 %all-reduce.64.cloned.1.call-start = ((), (), s32[]{:S(2)}) async-start(), calls=%async_computation.5 | async-start | bytes 1048576 | tf_op jit(solution)/shard_map/psum | solution.py:31
  253.3 97.4 %all-reduce.66.cloned.1.call-start = ((), (), s32[]{:S(2)}) async-start(), calls=%async_computation.6 | async-start | bytes 1048576 | tf_op jit(solution)/shard_map/psum | solution.py:31
  306.9 90.2 %all-reduce.68.cloned.1.call-start = ((), (), s32[]{:S(2)}) async-start(), calls=%async_computation.7 | async-start | bytes 1048576 | tf_op jit(solution)/shard_map/psum | solution.py:31
  350.7 97.5 %all-reduce.70.cloned.1.call-start = ((), (), s32[]{:S(2)}) async-start(), calls=%async_computation.8 | async-start | bytes 1048576 | tf_op jit(solution)/shard_map/psum | solution.py:31
  404.4 90.0 %all-reduce.72.cloned.1.call-start = ((), (), s32[]{:S(2)}) async-start(), calls=%async_computation.9 | async-start | bytes 1048576 | tf_op jit(solution)/shard_map/psum | solution.py:31
  448.3 97.3 %all-reduce.74.cloned.1.call-start = ((), (), s32[]{:S(2)}) async-start(), calls=%async_computation.10 | async-start | bytes 1048576 | tf_op jit(solution)/shard_map/psum | solution.py:31
  501.8 90.0 %all-reduce.76.cloned.1.call-start = ((), (), s32[]{:S(2)}) async-start(), calls=%async_computation.11 | async-start | bytes 1048576 | tf_op jit(solution)/shard_map/psum | solution.py:31
  545.6 97.4 %all-reduce.78.cloned.1.call-start = ((), (), s32[]{:S(2)}) async-start(), calls=%async_computation.12 | async-start | bytes 1048576 | tf_op jit(solution)/shard_map/psum | solution.py:31
  599.1 90.0 %all-reduce.80.cloned.1.call-start = ((), (), s32[]{:S(2)}) async-start(), calls=%async_computation.13 | async-start | bytes 1048576 | tf_op jit(solution)/shard_map/psum | solution.py:31
  643.0 97.4 %copy-start.6 = (s32[1,4,2]{1,2,0:T(2,128)S(1)}, s32[1,4,2]{1,2,0:T(2,128)}, u32[]{:S(2)}) copy-start(s32[1,4,2]{1,2,0:T(2,128)} %param.64) | copy-start | bytes 100
  643.0 97.5 %copy-start.5 = (f32[4,64,32]{1,2,0:T(8,128)S(1)}, f32[4,64,32]{1,2,0:T(8,128)}, u32[]{:S(2)}) copy-start(f32[4,64,32]{1,2,0:T(8,128)} %param.69) | copy-start | bytes 98308
  643.0 97.3 %all-reduce.82.cloned.1.call-start = ((), (), s32[]{:S(2)}) async-start(), calls=%async_computation.14 | async-start | bytes 1048576 | tf_op jit(solution)/shard_map/psum | solution.py:31
  696.5 90.0 %all-reduce.84.cloned.1.call-start = ((), (), s32[]{:S(2)}) async-start(), calls=%async_computation.15 | async-start | bytes 1048576 | tf_op jit(solution)/shard_map/psum | solution.py:31
  740.4 112.4 %all-reduce.86.cloned.1.call-start = ((), (), s32[]{:S(2)}) async-start(), calls=%async_computation.16 | async-start | bytes 524288 | tf_op jit(solution)/shard_map/psum | solution.py:73
  786.5 3.4 copy-start.1
  791.7 104.7 %all-reduce.88.cloned.1.call-start = ((), (), s32[]{:S(2)}) async-start(), calls=%async_computation.17 | async-start | bytes 524288 | tf_op jit(solution)/shard_map/psum | solution.py:31
  854.8 86.6 %all-reduce.90.cloned.1.call-start = ((), (), s32[]{:S(2)}) async-start(), calls=%async_computation.18 | async-start | bytes 524288 | tf_op jit(solution)/shard_map/psum | solution.py:31
  896.5 90.4 %all-reduce.92.cloned.1.call-start = ((), (), s32[]{:S(2)}) async-start(), calls=%async_computation.19 | async-start | bytes 524288 | tf_op jit(solution)/shard_map/psum | solution.py:31
  944.6 87.2 %all-reduce.94.cloned.1.call-start = ((), (), s32[]{:S(2)}) async-start(), calls=%async_computation.20 | async-start | bytes 524288 | tf_op jit(solution)/shard_map/psum | solution.py:31
  986.9 92.2 %all-reduce.96.cloned.1.call-start = ((), (), s32[]{:S(2)}) async-start(), calls=%async_computation.21 | async-start | bytes 524288 | tf_op jit(solution)/shard_map/psum | solution.py:31
  1036.8 87.3 %all-reduce.98.cloned.1.call-start = ((), (), s32[]{:S(2)}) async-start(), calls=%async_computation.22 | async-start | bytes 524288 | tf_op jit(solution)/shard_map/psum | solution.py:31
  1079.2 92.3 %all-reduce.100.cloned.1.call-start = ((), (), s32[]{:S(2)}) async-start(), calls=%async_computation.23 | async-start | bytes 524288 | tf_op jit(solution)/shard_map/psum | solution.py:31
  1127.1 272.5 %copy-start.4 = (f32[4,64,256]{2,1,0:T(8,128)S(1)}, f32[4,64,256]{2,1,0:T(8,128)}, u32[]{:S(2)}) copy-start(f32[4,64,256]{2,1,0:T(8,128)} %param.65) | copy-start | bytes 786436
  1129.1 87.3 %all-reduce.102.cloned.1.call-start = ((), (), s32[]{:S(2)}) async-start(), calls=%async_computation.24 | async-start | bytes 524288 | tf_op jit(solution)/shard_map/psum | solution.py:31
  1171.5 91.0 %all-reduce.104.cloned.1.call-start = ((), (), s32[]{:S(2)}) async-start(), calls=%async_computation.25 | async-start | bytes 524288 | tf_op jit(solution)/shard_map/psum | solution.py:31
  1220.1 87.2 %all-reduce.106.cloned.1.call-start = ((), (), s32[]{:S(2)}) async-start(), calls=%async_computation.26 | async-start | bytes 524288 | tf_op jit(solution)/shard_map/psum | solution.py:31
  1262.5 90.4 %all-reduce.108.cloned.1.call-start = ((), (), s32[]{:S(2)}) async-start(), calls=%async_computation.27 | async-start | bytes 524288 | tf_op jit(solution)/shard_map/psum | solution.py:31
  1310.6 87.4 %all-reduce.110.cloned.1.call-start = ((), (), s32[]{:S(2)}) async-start(), calls=%async_computation.28 | async-start | bytes 524288 | tf_op jit(solution)/shard_map/psum | solution.py:31
  1353.0 92.3 %all-reduce.112.cloned.1.call-start = ((), (), s32[]{:S(2)}) async-start(), calls=%async_computation.29 | async-start | bytes 524288 | tf_op jit(solution)/shard_map/psum | solution.py:31
  1402.9 87.3 %all-reduce.114.cloned.1.call-start = ((), (), s32[]{:S(2)}) async-start(), calls=%async_computation.30 | async-start | bytes 524288 | tf_op jit(solution)/shard_map/psum | solution.py:31
  1445.3 92.3 %all-reduce.116.cloned.1.call-start = ((), (), s32[]{:S(2)}) async-start(), calls=%async_computation.31 | async-start | bytes 524288 | tf_op jit(solution)/shard_map/psum | solution.py:31
  1495.2 87.2 %all-reduce.118.cloned.1.call-start = ((), (), s32[]{:S(2)}) async-start(), calls=%async_computation.32 | async-start | bytes 524288 | tf_op jit(solution)/shard_map/psum | solution.py:31
  1537.6 98.7 %all-reduce.120.cloned.1.call-start = ((), (), s32[]{:S(2)}) async-start(), calls=%async_computation.33 | async-start | bytes 1048576 | tf_op jit(solution)/shard_map/psum | solution.py:31
  1588.0 1.1 copy-start.2
  1592.7 89.9 %all-reduce.122.cloned.1.call-start = ((), (), s32[]{:S(2)}) async-start(), calls=%async_computation.34 | async-start | bytes 1048576 | tf_op jit(solution)/shard_map/psum | solution.py:31
  1636.3 99.2 %all-reduce.124.cloned.1.call-start = ((), (), s32[]{:S(2)}) async-start(), calls=%async_computation.35 | async-start | bytes 1048576 | tf_op jit(solution)/shard_map/psum | solution.py:31
  1691.7 90.0 %all-reduce.126.cloned.1.call-start = ((), (), s32[]{:S(2)}) async-start(), calls=%async_computation.36 | async-start | bytes 1048576 | tf_op jit(solution)/shard_map/psum | solution.py:31
  1735.6 101.1 %all-reduce.128.cloned.1.call-start = ((), (), s32[]{:S(2)}) async-start(), calls=%async_computation.37 | async-start | bytes 1048576 | tf_op jit(solution)/shard_map/psum | solution.py:31
  1792.9 90.0 %all-reduce.130.cloned.1.call-start = ((), (), s32[]{:S(2)}) async-start(), calls=%async_computation.38 | async-start | bytes 1048576 | tf_op jit(solution)/shard_map/psum | solution.py:31
  1836.7 101.2 %all-reduce.132.cloned.1.call-start = ((), (), s32[]{:S(2)}) async-start(), calls=%async_computation.39 | async-start | bytes 1048576 | tf_op jit(solution)/shard_map/psum | solution.py:31
  1894.1 90.2 %all-reduce.134.cloned.1.call-start = ((), (), s32[]{:S(2)}) async-start(), calls=%async_computation.40 | async-start | bytes 1048576 | tf_op jit(solution)/shard_map/psum | solution.py:31
  1937.9 101.3 %all-reduce.136.cloned.1.call-start = ((), (), s32[]{:S(2)}) async-start(), calls=%async_computation.41 | async-start | bytes 1048576 | tf_op jit(solution)/shard_map/psum | solution.py:31
  1995.4 90.0 %all-reduce.138.cloned.1.call-start = ((), (), s32[]{:S(2)}) async-start(), calls=%async_computation.42 | async-start | bytes 1048576 | tf_op jit(solution)/shard_map/psum | solution.py:31
  2039.2 101.1 %all-reduce.140.cloned.1.call-start = ((), (), s32[]{:S(2)}) async-start(), calls=%async_computation.43 | async-start | bytes 1048576 | tf_op jit(solution)/shard_map/psum | solution.py:31
  2096.5 90.0 %all-reduce.142.cloned.1.call-start = ((), (), s32[]{:S(2)}) async-start(), calls=%async_computation.44 | async-start | bytes 1048576 | tf_op jit(solution)/shard_map/psum | solution.py:31
  2140.4 101.1 %all-reduce.144.cloned.1.call-start = ((), (), s32[]{:S(2)}) async-start(), calls=%async_computation.45 | async-start | bytes 1048576 | tf_op jit(solution)/shard_map/psum | solution.py:31
  2197.7 90.0 %all-reduce.146.cloned.1.call-start = ((), (), s32[]{:S(2)}) async-start(), calls=%async_computation.46 | async-start | bytes 1048576 | tf_op jit(solution)/shard_map/psum | solution.py:31
  2241.6 101.2 %all-reduce.148.cloned.1.call-start = ((), (), s32[]{:S(2)}) async-start(), calls=%async_computation.47 | async-start | bytes 1048576 | tf_op jit(solution)/shard_map/psum | solution.py:31
  2298.9 90.0 %all-reduce.150.cloned.1.call-start = ((), (), s32[]{:S(2)}) async-start(), calls=%async_computation.48 | async-start | bytes 1048576 | tf_op jit(solution)/shard_map/psum | solution.py:31
Sparse Core Ops, SparseCore 0:
  16.0 45.5 all-reduce.53
  63.9 43.9 all-reduce.55
  113.3 42.6 all-reduce.57
  158.1 43.9 all-reduce.59
  209.6 43.6 all-reduce.61
  255.5 43.9 all-reduce.63
  307.0 43.6 all-reduce.65
  353.1 43.9 all-reduce.67
  404.5 43.6 all-reduce.69
  450.4 43.9 all-reduce.71
  501.9 43.6 all-reduce.73
  547.8 43.9 all-reduce.75
  599.3 43.6 all-reduce.77
  645.2 43.9 all-reduce.79
  696.6 43.6 all-reduce.81
  742.5 43.9 all-reduce.83
  791.8 60.8 all-reduce.85
  855.5 40.9 all-reduce.87
  898.8 42.5 all-reduce.89
  944.8 42.0 all-reduce.91
  989.2 42.5 all-reduce.93
  1036.9 42.2 all-reduce.95
  1081.5 42.5 all-reduce.97
  1129.2 42.2 all-reduce.99
  1173.8 42.5 all-reduce.101
  1220.3 42.2 all-reduce.103
  1264.7 42.5 all-reduce.105
  1310.7 42.2 all-reduce.107
  1355.3 42.5 all-reduce.109
  1403.0 42.2 all-reduce.111
  1447.6 42.5 all-reduce.113
  1495.3 42.2 all-reduce.115
  1539.8 42.5 all-reduce.117
  1592.8 43.4 all-reduce.119
  1638.6 43.9 all-reduce.121
  1691.8 43.6 all-reduce.123
  1737.8 43.9 all-reduce.125
  1793.0 43.6 all-reduce.127
  1838.9 43.9 all-reduce.129
  1894.2 43.6 all-reduce.131
  1940.2 43.9 all-reduce.133
  1995.5 43.6 all-reduce.135
  2041.4 43.9 all-reduce.137
  2096.7 43.6 all-reduce.139
  2142.6 43.9 all-reduce.141
  2197.8 43.6 all-reduce.143
  2243.8 43.9 all-reduce.145
  2299.0 43.6 all-reduce.147
  2344.9 43.9 all-reduce.149
